TPU v7x, 256 devices: a whole 4x4x8 slice. The times are simulated.
256 devices in a mesh: dp: 8 (over z), ctx: 32 (over x, y, core).
Axes of the slice: x: 4, y: 4, z: 8, core: 2. Of those that a mesh axis runs over, the one named last changes fastest.
Arguments:
- queries: bfloat16 [8, 4096, 4096], P('dp', 'ctx')
- keys: bfloat16 [8, 4096, 4096], P('dp', 'ctx')
- values: bfloat16 [8, 4096, 4096], P('dp', 'ctx'), may hold values from -6 to 6
- d_out: bfloat16 [8, 4096, 4096], P('dp', 'ctx'), may hold values from -6 to 6
- gains: float32 [2, 4096], P(None, 'dp'), may hold values from 0.5 to 2
- window_widths: int32 [32], P('ctx'), may hold values from 0 to 1
- global_blocks: int32 [8, 2], P('dp'), may hold values from 0 to 31, as said below
- random_blocks: int32 [8, 32, 3], P('dp'), may hold values from 0 to 31
Outputs:
- out: bfloat16 [8, 4096, 4096], P('dp', 'ctx')
- d_queries: bfloat16 [8, 4096, 4096], P('dp', 'ctx')
- d_keys: bfloat16 [8, 4096, 4096], P('dp', 'ctx')
- d_values: bfloat16 [8, 4096, 4096], P('dp', 'ctx')
- d_gains: float32 [2, 4096], P(None, 'dp')
Inputs may be any that keep to these rules, and one draw needn't show every extreme that they name: `global_blocks`: the 2 ids of a sequence are different.
All inputs are finite; a program needn't handle non-finite values.
Results may differ from a plain program's by a relative error of at most 0.018.
The roundings to bfloat16 on the way count: a program that leaves them out, or rounds other values in their place, can miss the bound.
Values may be sent and summed in bfloat16 or wider, within the bound.
No kernel may reach another device: no remote copies, remote signals or barrier semaphores. Data moves between devices by JAX's collectives and lax.ppermute only.
A program may use at most 128 MiB of HBM per device.

v0:
```python
import math
import jax
import jax.numpy as jnp
from jax import lax
from jax.sharding import PartitionSpec as P

HD = 128
WMAX = 1
NEG_FILL = -1e30


def slot_table(global_ids, random_ids, widths):
    block_count = random_ids.shape[0]
    blocks = jnp.arange(block_count, dtype=jnp.int32)
    offsets = jnp.arange(-WMAX, WMAX + 1, dtype=jnp.int32)
    nearby = blocks[:, None] + offsets[None, :]
    inside = (nearby >= 0) & (nearby < block_count)
    in_window = jnp.abs(offsets)[None, :] <= widths[:, None]
    window_ok = inside[None, :, :] & in_window[:, None, :]
    global_cols = jnp.broadcast_to(global_ids[None, :], (block_count, global_ids.shape[0]))
    slot_ids = jnp.concatenate([nearby, global_cols, random_ids], axis=1)
    always_on = jnp.ones(
        (widths.shape[0], block_count, global_ids.shape[0] + random_ids.shape[1]), dtype=jnp.bool_
    )
    listed = jnp.concatenate([window_ok, always_on], axis=2)
    slot_total = slot_ids.shape[1]
    matches = slot_ids[:, :, None] == slot_ids[:, None, :]
    position = jnp.arange(slot_total)
    earlier = position[None, :] < position[:, None]
    repeated = jnp.any(matches[None] & earlier[None, None] & listed[:, :, None, :], axis=3)
    usable = listed & jnp.logical_not(repeated)
    return (jnp.clip(slot_ids, 0, block_count - 1), usable)


def softmax_rows(scores):
    row_max = jnp.max(scores, axis=-1, keepdims=True)
    exponent = jnp.exp(scores - row_max)
    return exponent / jnp.sum(exponent, axis=-1, keepdims=True)


def slot_weights(q_group, k_slots, usable_group, block_len, score_scale):
    scores = (
        jnp.einsum("irhd,ijhd->ihrj", q_group, k_slots, preferred_element_type=jnp.float32)
        * score_scale
    )
    allowed = jnp.repeat(usable_group, block_len, axis=2)
    return softmax_rows(jnp.where(allowed[:, :, None, :], scores, NEG_FILL))


def gather_slots(blocks_in, id_group):
    group_len, slot_total = id_group.shape
    picked = blocks_in[id_group]
    return picked.reshape(group_len, slot_total * picked.shape[2], picked.shape[3], picked.shape[4])


def group_layout(block_count, block_len):
    group_len = math.gcd(block_count, max(1, 512 // block_len))
    return (group_len, block_count // group_len)


def forward_pass(q_blocks, k_blocks, v_blocks, slot_ids, usable_t, global_ids, score_scale):
    block_count, block_len, head_count, head_dim = q_blocks.shape
    group_len, step_count = group_layout(block_count, block_len)

    def forward_one_group(running, inputs_now):
        q_group, id_group, usable_group = inputs_now
        k_slots = gather_slots(k_blocks, id_group)
        v_slots = gather_slots(v_blocks, id_group)
        weights_b = slot_weights(q_group, k_slots, usable_group, block_len, score_scale).astype(
            jnp.bfloat16
        )
        attended = jnp.einsum(
            "ihrj,ijhd->irhd", weights_b, v_slots, preferred_element_type=jnp.float32
        )
        return (running, attended.astype(jnp.bfloat16))

    split_inputs = (
        q_blocks.reshape(step_count, group_len, block_len, head_count, head_dim),
        slot_ids.reshape(step_count, group_len, -1),
        usable_t.reshape(step_count, group_len, head_count, -1),
    )
    _, attended = lax.scan(forward_one_group, jnp.zeros((), jnp.int32), split_inputs)
    attended = attended.reshape(block_count, block_len, head_count, head_dim)
    k_flat = k_blocks.reshape(block_count * block_len, head_count, head_dim)
    v_flat = v_blocks.reshape(block_count * block_len, head_count, head_dim)
    full_w = softmax_rows(
        jnp.einsum(
            "grhd,thd->ghrt", q_blocks[global_ids], k_flat, preferred_element_type=jnp.float32
        )
        * score_scale
    )
    full_out = jnp.einsum(
        "ghrt,thd->grhd", full_w.astype(jnp.bfloat16), v_flat, preferred_element_type=jnp.float32
    )
    return attended.at[global_ids].set(full_out.astype(jnp.bfloat16))


def backward_pass(
    q_blocks, k_blocks, v_blocks, out_blocks, d_blocks, slot_ids, usable_t, global_ids, score_scale
):
    block_count, block_len, head_count, head_dim = q_blocks.shape
    group_len, step_count = group_layout(block_count, block_len)
    row_dot = jnp.sum(d_blocks.astype(jnp.float32) * out_blocks.astype(jnp.float32), axis=3)
    is_global = jnp.any(jnp.arange(block_count)[:, None] == global_ids[None, :], axis=1)
    d_rows = jnp.where(is_global[:, None, None, None], jnp.zeros((), jnp.bfloat16), d_blocks)
    dot_rows = jnp.where(is_global[:, None, None], jnp.zeros((), jnp.float32), row_dot)

    def backward_one_group(running, inputs_now):
        dk_sum, dv_sum = running
        q_group, d_group, dot_group, id_group, usable_group = inputs_now
        k_slots = gather_slots(k_blocks, id_group)
        v_slots = gather_slots(v_blocks, id_group)
        weights = slot_weights(q_group, k_slots, usable_group, block_len, score_scale)
        weights_b = weights.astype(jnp.bfloat16)
        d_weights = jnp.einsum(
            "irhd,ijhd->ihrj", d_group, v_slots, preferred_element_type=jnp.float32
        )
        d_scores = (weights * (d_weights - jnp.transpose(dot_group, (0, 2, 1))[..., None])).astype(
            jnp.bfloat16
        )
        dq_group = (
            jnp.einsum("ihrj,ijhd->irhd", d_scores, k_slots, preferred_element_type=jnp.float32)
            * score_scale
        )
        slot_rows = id_group.shape[0] * id_group.shape[1]
        dk_slots = (
            jnp.einsum("ihrj,irhd->ijhd", d_scores, q_group, preferred_element_type=jnp.float32)
            * score_scale
        ).reshape(slot_rows, block_len, head_count, head_dim)
        dv_slots = jnp.einsum(
            "ihrj,irhd->ijhd", weights_b, d_group, preferred_element_type=jnp.float32
        ).reshape(slot_rows, block_len, head_count, head_dim)
        flat_ids = id_group.reshape(-1)
        return ((dk_sum.at[flat_ids].add(dk_slots), dv_sum.at[flat_ids].add(dv_slots)), dq_group)

    empty = jnp.zeros((block_count, block_len, head_count, head_dim), jnp.float32)
    split_inputs = (
        q_blocks.reshape(step_count, group_len, block_len, head_count, head_dim),
        d_rows.reshape(step_count, group_len, block_len, head_count, head_dim),
        dot_rows.reshape(step_count, group_len, block_len, head_count),
        slot_ids.reshape(step_count, group_len, -1),
        usable_t.reshape(step_count, group_len, head_count, -1),
    )
    (dk_blocks, dv_blocks), dq_blocks = lax.scan(backward_one_group, (empty, empty), split_inputs)
    dq_blocks = dq_blocks.reshape(block_count, block_len, head_count, head_dim)
    length = block_count * block_len
    flat_shape = (length, head_count, head_dim)
    k_flat = k_blocks.reshape(flat_shape)
    v_flat = v_blocks.reshape(flat_shape)
    q_global = q_blocks[global_ids]
    d_global = d_blocks[global_ids]
    full_w = softmax_rows(
        jnp.einsum("grhd,thd->ghrt", q_global, k_flat, preferred_element_type=jnp.float32)
        * score_scale
    )
    full_b = full_w.astype(jnp.bfloat16)
    d_full = jnp.einsum("grhd,thd->ghrt", d_global, v_flat, preferred_element_type=jnp.float32)
    full_scores = (
        full_w * (d_full - jnp.transpose(row_dot[global_ids], (0, 2, 1))[..., None])
    ).astype(jnp.bfloat16)
    dq_blocks = dq_blocks.at[global_ids].add(
        jnp.einsum("ghrt,thd->grhd", full_scores, k_flat, preferred_element_type=jnp.float32)
        * score_scale
    )
    dq_all = dq_blocks.reshape(flat_shape)
    dk_all = (
        dk_blocks.reshape(flat_shape)
        + jnp.einsum("ghrt,grhd->thd", full_scores, q_global, preferred_element_type=jnp.float32)
        * score_scale
    )
    dv_all = dv_blocks.reshape(flat_shape) + jnp.einsum(
        "ghrt,grhd->thd", full_b, d_global, preferred_element_type=jnp.float32
    )
    return (dq_all, dk_all, dv_all)


def on_device(queries, keys, values, d_out, gains, window_widths, global_blocks, random_blocks):
    head_count = window_widths.shape[0]
    width_dev = head_count * HD
    global_ids = global_blocks[0]
    random_ids = random_blocks[0]
    block_count = random_ids.shape[0]
    score_scale = 1.0 / math.sqrt(HD)
    all_gains = lax.all_gather(gains, "dp", axis=1, tiled=True)
    own_gains = lax.dynamic_slice_in_dim(all_gains, lax.axis_index("ctx") * width_dev, width_dev, 1)
    gain_q = own_gains[0].reshape(head_count, HD)
    gain_k = own_gains[1].reshape(head_count, HD)
    q_heads, k_heads, v_heads = (
        lax.all_to_all(queries[0], "ctx", split_axis=1, concat_axis=0, tiled=True),
        lax.all_to_all(keys[0], "ctx", split_axis=1, concat_axis=0, tiled=True),
        lax.all_to_all(values[0], "ctx", split_axis=1, concat_axis=0, tiled=True),
    )
    length = q_heads.shape[0]
    block_len = length // block_count
    flat_shape = (length, head_count, HD)
    block_shape = (block_count, block_len, head_count, HD)
    q_scaled = (q_heads.reshape(flat_shape).astype(jnp.float32) * gain_q).astype(jnp.bfloat16)
    k_scaled = (k_heads.reshape(flat_shape).astype(jnp.float32) * gain_k).astype(jnp.bfloat16)
    slot_ids, usable = slot_table(global_ids, random_ids, window_widths)
    usable_t = jnp.transpose(usable, (1, 0, 2))
    out_blocks = forward_pass(
        q_scaled.reshape(block_shape),
        k_scaled.reshape(block_shape),
        v_heads.reshape(block_shape),
        slot_ids,
        usable_t,
        global_ids,
        score_scale,
    )
    out_tokens = lax.all_to_all(
        out_blocks.reshape(length, width_dev), "ctx", split_axis=0, concat_axis=1, tiled=True
    )
    d_heads = lax.all_to_all(d_out[0], "ctx", split_axis=1, concat_axis=0, tiled=True)
    q_back, k_back, v_back = (q_heads, k_heads, v_heads)
    q_back_scaled, k_back_scaled = (q_scaled, k_scaled)
    dq_all, dk_all, dv_all = backward_pass(
        q_back_scaled.reshape(block_shape),
        k_back_scaled.reshape(block_shape),
        v_back.reshape(block_shape),
        out_blocks,
        d_heads.reshape(block_shape),
        slot_ids,
        usable_t,
        global_ids,
        score_scale,
    )
    grad_q = (dq_all * gain_q).astype(jnp.bfloat16).reshape(length, width_dev)
    grad_k = (dk_all * gain_k).astype(jnp.bfloat16).reshape(length, width_dev)
    grad_v = dv_all.astype(jnp.bfloat16).reshape(length, width_dev)
    back_q, back_k, back_v = (
        lax.all_to_all(grad_q, "ctx", split_axis=0, concat_axis=1, tiled=True),
        lax.all_to_all(grad_k, "ctx", split_axis=0, concat_axis=1, tiled=True),
        lax.all_to_all(grad_v, "ctx", split_axis=0, concat_axis=1, tiled=True),
    )
    gain_terms = jnp.stack(
        [
            jnp.sum(dq_all * q_back.reshape(flat_shape).astype(jnp.float32), axis=0),
            jnp.sum(dk_all * k_back.reshape(flat_shape).astype(jnp.float32), axis=0),
        ]
    ).reshape(2, width_dev)
    columns = lax.all_gather(gain_terms, "ctx", axis=1, tiled=True)
    d_gains = lax.psum_scatter(
        columns.astype(jnp.bfloat16), "dp", scatter_dimension=1, tiled=True
    ).astype(jnp.float32)
    return (out_tokens[None], back_q[None], back_k[None], back_v[None], d_gains)


def solution(mesh):
    placed = (
        P("dp", "ctx", None),
        P("dp", "ctx", None),
        P("dp", "ctx", None),
        P("dp", "ctx", None),
        P(None, "dp"),
        P("ctx"),
        P("dp", None),
        P("dp", None, None),
    )
    return jax.shard_map(
        on_device,
        mesh=mesh,
        in_specs=placed,
        out_specs=(
            P("dp", "ctx", None),
            P("dp", "ctx", None),
            P("dp", "ctx", None),
            P("dp", "ctx", None),
            P(None, "dp"),
        ),
        check_vma=False,
    )
```

profile of v0, /device:TPU:2, one launch (start us, length us, event | category | flops | bytes accessed | tf_op | source)
XLA Modules:
  0.0 676.2 jit_solution(1531738499549589078)
XLA Ops:
  10.1 7.6 %all-to-all-start.1 = ((bf16[128,32,128]{2,0,1:T(8,128)(2,1)}), bf16[128,32,128]{2,0,1:T(8,128)(2,1)S(1)}, u32[]{:S(2)}, u32[]{:S(2)}) async-start(bf16[128,32,128]{2,0,1:T(8,128)(2,1)} %copy.222), calls=%async_computation.1 | async-start | bytes 2097152 | tf_op jit(solution)/shard_map/all_to_all | solution.py:189
  19.1 13.1 %all-to-all-done.1 = bf16[128,32,128]{2,0,1:T(8,128)(2,1)S(1)} async-done(((bf16[128,32,128]{2,0,1:T(8,128)(2,1)}), bf16[128,32,128]{2,0,1:T(8,128)(2,1)S(1)}, u32[]{:S(2)}, u32[]{:S(2)}) %all-to-all-start.1) | async-done | bytes 1048608 | tf_op jit(solution)/shard_map/all_to_all | solution.py:189
  32.2 6.6 all-to-all-start.2
  41.1 12.1 %all-to-all-done.2 = bf16[128,32,128]{0,2,1:T(8,128)(2,1)S(1)} async-done(((bf16[128,32,128]{0,2,1:T(8,128)(2,1)}), bf16[128,32,128]{0,2,1:T(8,128)(2,1)S(1)}, u32[]{:S(2)}, u32[]{:S(2)}) %all-to-all-start.2) | async-done | bytes 1048608 | tf_op jit(solution)/shard_map/all_to_all | solution.py:190
  53.2 6.4 all-to-all-start
  65.5 8.5 %all-to-all-done = bf16[128,32,128]{0,2,1:T(8,128)(2,1)S(1)} async-done(((bf16[128,32,128]{0,2,1:T(8,128)(2,1)}), bf16[128,32,128]{0,2,1:T(8,128)(2,1)S(1)}, u32[]{:S(2)}, u32[]{:S(2)}) %all-to-all-start) | async-done | bytes 1048608 | tf_op jit(solution)/shard_map/all_to_all | solution.py:191
  75.0 6.4 all-to-all-start.4
  81.5 28.3 %all_gather.6 = f32[2,4096]{1,0:T(2,128)S(1)} all-gather(f32[2,512]{1,0:T(2,128)S(1)} %copy-done.23), channel_id=1, replica_groups=mesh['dp'=8,'ctx'=32] {'dp'}, dimensions={1}, use_global_device_ids=true | all-gather | bytes 36864 | tf_op jit(solution)/shard_map/all_gather | solution.py:184
  125.8 76.6 %while.24 = (s32[]{:T(128)}, bf16[8,4,128,1,128]{4,2,1,0,3:T(8,128)(2,1)}, s32[8,4,8]{2,1,0:T(4,128)S(1)}, bf16[32,128,1,128]{3,1,0,2:T(8,128)(2,1)S(1)}, pred[8...) while((s32[]{:T(128)}, ...), condition=%wide.region_4.5_spmd, body=%wide.region_1.4_spmd.sunk | while | flops 271648864 | bytes 11297869 | solution.py:82
  129.4 3.0 fusion.131
  139.0 3.0 fusion.131
  148.6 3.0 fusion.131
  158.2 3.0 fusion.131
  167.7 3.0 fusion.131
  177.3 3.0 fusion.131
  186.9 3.0 fusion.131
  196.5 3.0 fusion.131
  213.3 3.4 fusion.56
  224.2 292.6 %while.25 = (s32[]{:T(128)}, f32[32,128,1,128]{3,1,0,2:T(8,128)}, f32[32,128,1,128]{3,1,0,2:T(8,128)}, f32[8,4,128,1,128]{4,2,1,0,3:T(8,128)}, s32[8,4,8]{2,1,0:...) while((s32[]{:T(128)}, f32[32,128,1,128]{3,1,0,2:T(8,128)}, ...), condition=%wide.region_15.16_spmd, body=%wide.region_10.15_spmd.sunk | while | flops 677972160 | bytes 57460872 | solution.py:144
  229.1 3.0 fusion.144
  236.8 2.8 convolution_bitcast_fusion.5
  241.4 6.4 scatter_fusion.1
  248.6 3.1 multiply_bitcast_fusion.2
  253.7 6.5 scatter_fusion
  265.8 3.0 fusion.144
  273.5 2.8 convolution_bitcast_fusion.5
  278.2 6.3 scatter_fusion.1
  285.3 3.1 multiply_bitcast_fusion.2
  290.3 6.3 scatter_fusion
  302.3 3.0 fusion.144
  314.7 6.3 scatter_fusion.1
  321.8 3.1 multiply_bitcast_fusion.2
  326.8 6.4 scatter_fusion
  338.9 3.0 fusion.144
  351.3 6.2 scatter_fusion.1
  358.3 3.1 multiply_bitcast_fusion.2
  363.4 6.4 scatter_fusion
  375.4 3.0 fusion.144
  387.8 6.2 scatter_fusion.1
  394.8 3.1 multiply_bitcast_fusion.2
  399.9 6.4 scatter_fusion
  411.9 3.0 fusion.144
  424.3 6.3 scatter_fusion.1
  431.4 3.1 multiply_bitcast_fusion.2
  436.5 6.4 scatter_fusion
  448.5 3.0 fusion.144
  460.8 6.3 scatter_fusion.1
  468.0 3.1 multiply_bitcast_fusion.2
  473.0 6.4 scatter_fusion
  485.1 3.0 fusion.144
  492.7 2.8 convolution_bitcast_fusion.5
  497.4 6.3 scatter_fusion.1
  504.5 3.1 multiply_bitcast_fusion.2
  509.6 6.5 scatter_fusion
  521.7 21.9 %all_to_all.119 = bf16[32,128,128]{2,1,0:T(8,128)(2,1)} all-to-all(bf16[32,128,128]{2,1,0:T(8,128)(2,1)S(1)} %get-tuple-element.281), channel_id=1, replica_groups=mesh['dp'=8,'ctx'=32] {'ctx'}, dimensions={0} | all-to-all | bytes 2097152 | tf_op jit(solution)/shard_map/all_to_all | solution.py:231
  543.5 6.4 all-to-all-start.3
  555.3 3.1 copy.271
  558.4 3.2 multiply_reduce_fusion.1
  564.4 6.9 %all-to-all-start.6 = ((bf16[32,128,128]{1,2,0:T(8,128)(2,1)}), bf16[32,128,128]{1,2,0:T(8,128)(2,1)}, u32[]{:S(2)}, u32[]{:S(2)}) async-start(bf16[32,128,128]{1,2,0:T(8,128)(2,1)} %copy.248), calls=%async_computation.6 | async-start | bytes 2097152 | tf_op jit(solution)/shard_map/all_to_all | solution.py:232
  571.3 3.1 copy.272
  578.5 7.4 %all-to-all-done.6 = bf16[32,128,128]{1,2,0:T(8,128)(2,1)} async-done(((bf16[32,128,128]{1,2,0:T(8,128)(2,1)}), bf16[32,128,128]{1,2,0:T(8,128)(2,1)}, u32[]{:S(2)}, u32[]{:S(2)}) %all-to-all-start.6) | async-done | bytes 1048608 | tf_op jit(solution)/shard_map/all_to_all | solution.py:232
  585.9 6.4 all-to-all-start.7
  592.3 29.2 %all-gather = bf16[2,1,4096]{2,1,0:T(2,128)(2,1)S(1)} all-gather(bf16[2,1,128]{2,1,0:T(2,128)(2,1)S(1)} %pad_maximum_fusion), channel_id=2, replica_groups=mesh['dp'=8,'ctx'=32] {'ctx'}, dimensions={2}, use_global_device_ids=true | all-gather | bytes 16896 | tf_op jit(solution)/shard_map/all_gather | solution.py:241
  622.9 35.8 %reduce-scatter.4.cloned.1.call-done = bf16[512,2]{1,0:T(8,128)(2,1)} async-done(((bf16[4096,2]{1,0:T(8,128)(2,1)}), bf16[512,2]{1,0:T(8,128)(2,1)}) %reduce-scatter.4.cloned.1.call-update) | async-done | bytes 2064
  (435 shorter events, 261.8 us)
Async XLA Ops:
  8.8 9.0 %copy-start.16 = (bf16[1,128,4096]{2,1,0:T(8,128)(2,1)S(1)}, bf16[1,128,4096]{2,1,0:T(8,128)(2,1)}, u32[]{:S(2)}) copy-start(bf16[1,128,4096]{2,1,0:T(8,128)(2,1)} %param.13) | copy-start | bytes 3145732
  10.1 22.1 %all-to-all-start.1 = ((bf16[128,32,128]{2,0,1:T(8,128)(2,1)}), bf16[128,32,128]{2,0,1:T(8,128)(2,1)S(1)}, u32[]{:S(2)}, u32[]{:S(2)}) async-start(bf16[128,32,128]{2,0,1:T(8,128)(2,1)} %copy.222), calls=%async_computation.1 | async-start | bytes 2097152 | tf_op jit(solution)/shard_map/all_to_all | solution.py:189
  17.8 21.7 %copy-start.21 = (s32[1,32,3]{1,0,2:T(1,128)S(1)}, s32[1,32,3]{1,0,2:T(1,128)}, u32[]{:S(2)}) copy-start(s32[1,32,3]{1,0,2:T(1,128)} %param.19) | copy-start | bytes 1156
  19.1 20.4 %copy-start.17 = (bf16[1,128,4096]{2,1,0:T(8,128)(2,1)S(1)}, bf16[1,128,4096]{2,1,0:T(8,128)(2,1)}, u32[]{:S(2)}) copy-start(bf16[1,128,4096]{2,1,0:T(8,128)(2,1)} %param.14) | copy-start | bytes 3145732
  32.2 82.9 %copy-start.8 = (bf16[128,32,128]{2,0,1:T(8,128)(2,1)}, bf16[128,32,128]{2,0,1:T(8,128)(2,1)S(1)}, u32[]{:S(2)}) copy-start(bf16[128,32,128]{2,0,1:T(8,128)(2,1)S(1)} %all-to-all-done.1) | copy-start | bytes 3145732
  32.2 8.7 %copy-start.24 = (s32[1,2]{1,0:T(1,128)S(1)}, s32[1,2]{1,0:T(1,128)}, u32[]{:S(2)}) copy-start(s32[1,2]{1,0:T(1,128)} %param.18) | copy-start | bytes 28
  32.2 21.0 %all-to-all-start.2 = ((bf16[128,32,128]{0,2,1:T(8,128)(2,1)}), bf16[128,32,128]{0,2,1:T(8,128)(2,1)S(1)}, u32[]{:S(2)}, u32[]{:S(2)}) async-start(bf16[128,32,128]{0,2,1:T(8,128)(2,1)} %bitcast.47), calls=%async_computation.2 | async-start | bytes 2097152 | tf_op jit(solution)/shard_map/all_to_all | solution.py:190
  53.2 56.6 %copy-start.11 = (bf16[128,32,128]{0,2,1:T(8,128)(2,1)}, bf16[128,32,128]{0,2,1:T(8,128)(2,1)S(1)}, u32[]{:S(2)}) copy-start(bf16[128,32,128]{0,2,1:T(8,128)(2,1)S(1)} %all-to-all-done.2) | copy-start | bytes 3145732
  53.2 20.9 %all-to-all-start = ((bf16[128,32,128]{0,2,1:T(8,128)(2,1)}), bf16[128,32,128]{0,2,1:T(8,128)(2,1)S(1)}, u32[]{:S(2)}, u32[]{:S(2)}) async-start(bf16[128,32,128]{0,2,1:T(8,128)(2,1)} %bitcast.378), calls=%async_computation | async-start | bytes 2097152 | tf_op jit(solution)/shard_map/all_to_all | solution.py:191
  63.2 18.2 %copy-start.23 = (f32[2,512]{1,0:T(2,128)S(1)}, f32[2,512]{1,0:T(2,128)}, u32[]{:S(2)}) copy-start(f32[2,512]{1,0:T(2,128)} %param.16) | copy-start | bytes 12292
  65.5 143.4 %copy-start.22 = (s32[2]{0:T(128)}, s32[2]{0:T(128)S(1)}, u32[]{:S(2)}) copy-start(s32[2]{0:T(128)S(1)} %fusion.87) | copy-start | bytes 28
  74.1 1.0 copy-start.15
  75.0 43.1 %all-to-all-start.4 = ((bf16[128,32,128]{2,0,1:T(8,128)(2,1)}), bf16[128,32,128]{2,0,1:T(8,128)(2,1)S(1)}, u32[]{:S(2)}, u32[]{:S(2)}) async-start(bf16[128,32,128]{2,0,1:T(8,128)(2,1)} %copy.234), calls=%async_computation.4 | async-start | bytes 2097152 | tf_op jit(solution)/shard_map/all_to_all | solution.py:213
  109.8 14.8 %copy-start.20 = (f32[128]{0:T(128)}, f32[128]{0:T(128)S(1)}, u32[]{:S(2)}) copy-start(f32[128]{0:T(128)S(1)} %get-tuple-element.285) | copy-start | bytes 1540
  109.8 106.9 %copy-start.18 = (f32[128]{0:T(128)}, f32[128]{0:T(128)S(1)}, u32[]{:S(2)}) copy-start(f32[128]{0:T(128)S(1)} %get-tuple-element.284) | copy-start | bytes 1540
  118.1 1.0 copy-start.9
  121.1 2.0 copy-start.5
  204.9 1.9 copy-start.1
  207.6 1.3 copy-start.2
  207.6 3.3 copy-start.10
  213.3 4.8 copy-start.7
  216.7 1.3 copy-start.12
  232.1 0.6 copy-start.26
  234.8 1.0 copy-start
  234.8 2.0 copy-start.25
  234.8 2.0 copy-start.27
  253.7 6.5 copy-start.4
  271.5 1.0 copy-start
  271.5 2.0 copy-start.25
  271.5 2.0 copy-start.27
  290.3 6.3 copy-start.4
  308.0 1.0 copy-start
  308.0 2.0 copy-start.25
  308.0 2.0 copy-start.27
  326.8 6.4 copy-start.4
  344.6 1.0 copy-start
  344.6 2.0 copy-start.25
  344.6 2.0 copy-start.27
  363.4 6.4 copy-start.4
  381.1 1.0 copy-start
  381.1 2.0 copy-start.25
  381.1 2.0 copy-start.27
  399.9 6.4 copy-start.4
  417.6 1.0 copy-start
  417.6 2.0 copy-start.25
  417.6 2.0 copy-start.27
  436.4 6.4 copy-start.4
  454.2 1.0 copy-start
  454.2 2.0 copy-start.25
  454.2 2.0 copy-start.27
  473.0 6.4 copy-start.4
  490.8 1.0 copy-start
  490.8 2.0 copy-start.25
  490.8 2.0 copy-start.27
  509.6 6.5 copy-start.4
  521.7 28.3 %copy-start.6 = (f32[32,128,128]{1,2,0:T(8,128)S(1)}, f32[32,128,128]{1,2,0:T(8,128)}, u32[]{:S(2)}) copy-start(f32[32,128,128]{1,2,0:T(8,128)} %copy-done.5) | copy-start | bytes 6291460
  543.5 20.9 %all-to-all-start.3 = ((bf16[32,128,128]{2,1,0:T(8,128)(2,1)}), bf16[32,128,128]{2,1,0:T(8,128)(2,1)S(1)}, u32[]{:S(2)}, u32[]{:S(2)}) async-start(bf16[32,128,128]{2,1,0:T(8,128)(2,1)} %scatter_fusion.2), calls=%async_computation.3 | async-start | bytes 2097152 | tf_op jit(solution)/shard_map/all_to_all | solution.py:210
  555.3 3.1 copy-start.13
  555.3 3.1 copy-start.19
  564.4 21.5 %all-to-all-start.6 = ((bf16[32,128,128]{1,2,0:T(8,128)(2,1)}), bf16[32,128,128]{1,2,0:T(8,128)(2,1)}, u32[]{:S(2)}, u32[]{:S(2)}) async-start(bf16[32,128,128]{1,2,0:T(8,128)(2,1)} %copy.248), calls=%async_computation.6 | async-start | bytes 2097152 | tf_op jit(solution)/shard_map/all_to_all | solution.py:232
  571.3 3.1 copy-start.3
  578.5 81.8 %copy-start.14 = (bf16[32,128,128]{2,1,0:T(8,128)(2,1)S(1)}, bf16[32,128,128]{2,1,0:T(8,128)(2,1)}, u32[]{:S(2)}) copy-start(bf16[32,128,128]{2,1,0:T(8,128)(2,1)} %all_to_all.119) | copy-start | bytes 3145732
  585.9 82.2 %all-to-all-start.7 = ((bf16[32,128,128]{1,2,0:T(8,128)(2,1)}), bf16[32,128,128]{1,2,0:T(8,128)(2,1)S(1)}, u32[]{:S(2)}, u32[]{:S(2)}) async-start(bf16[32,128,128]{1,2,0:T(8,128)(2,1)} %copy.252), calls=%async_computation.7 | async-start | bytes 2097152 | tf_op jit(solution)/shard_map/all_to_all | solution.py:233
  592.3 66.4 %reduce-scatter.4.cloned.1.call-start = ((), (), s32[]{:S(2)}) async-start(), calls=%async_computation.9 | async-start | bytes 1179648
  (7 other events, 3.9 us)
Sparse Core Ops, SparseCore 0:
  623.0 35.6 reduce-scatter.3
where the time goes:
time: 683 us; the launch traced here: 676 us
  local copies, waits for them, and re-layouts  185 us (27%)
  matrix products  147 us (22%)
  other arithmetic  124 us (18%)
  blocking collectives  79.3 us (12%)
  waiting for transfers between devices  78.1 us (11%)
  starting transfers between devices  46.8 us (7%)
  between operations  15.1 us (2%)
    scatter-add x8, other arithmetic, backward_one_group(): dk_sum.at[flat_ids].add(dk_slots)  51.1 us
    scatter-add x8, other arithmetic, backward_one_group(): dv_sum.at[flat_ids].add(dv_slots)  50.3 us
    sub x16, matrix products, softmax_rows(): exponent = jnp.exp(scores - row_max)  47.9 us
    gather x32, local copies, waits for them, and re-layouts, gather_slots(): picked = blocks_in[id_group]  43.5 us
    unnamed x2, waiting for transfers between devices  35.8 us
    all_gather x1, blocking collectives, on_device(): columns = lax.all_gather(gain_terms, 'ctx', axis=1, tiled=True)  29.2 us
    all_gather x1, blocking collectives, on_device(): all_gains = lax.all_gather(gains, 'dp', axis=1, tiled=True)  28.3 us
    dot_general x8, matrix products, backward_one_group(): jnp.einsum('ihrj,irhd->ijhd', d_scores, q_group, preferred_element_type=j...  25.1 us
  transfers between devices with their start and end apart: 8, of which 6 were waited for; matrix products, arithmetic and copies ran while one was open for 7% of the time, Pallas kernels for 0%

commit v1 on v0

--- a/solution.py
+++ b/solution.py
@@ -228,7 +228,10 @@
     grad_k = (dk_all * gain_k).astype(jnp.bfloat16).reshape(length, width_dev)
     grad_v = dv_all.astype(jnp.bfloat16).reshape(length, width_dev)
     back_q, back_k, back_v = (
-        lax.all_to_all(grad_q, "ctx", split_axis=0, concat_axis=1, tiled=True),
+        jnp.concatenate(
+            lax.all_to_all(jnp.stack(jnp.split(grad_q, lax.axis_size("ctx"), axis=0)), "ctx", 0, 0),
+            axis=1,
+        ),
         lax.all_to_all(grad_k, "ctx", split_axis=0, concat_axis=1, tiled=True),
         lax.all_to_all(grad_v, "ctx", split_axis=0, concat_axis=1, tiled=True),
     )

time: 683 us -> 687 us (level)
  blocking collectives: 79.3 us -> 56.6 us
  local copies, waits for them, and re-layouts: 185 us -> 202 us
  starting transfers between devices: 46.8 us -> 56.7 us
    all_to_all x1 -> x0, blocking collectives: 21.9 us -> none  [on_device(): lax.all_to_all(grad_q, 'ctx', split_axis=0, concat_axis=1, tiled=True)]
    unnamed x59 -> x89, local copies, waits for them, and re-layouts: 21.8 us -> 36.8 us
    all_to_all x1, waiting for transfers between devices: 12.1 us -> 0.01 us  [on_device(): lax.all_to_all(keys[0], 'ctx', split_axis=1, concat_axis=0, tiled=True)]
    all_to_all x0 -> x1, waiting for transfers between devices: none -> 7.4 us  [on_device(): lax.all_to_all(jnp.stack(jnp.split(grad_q, lax.axis_size('ctx'), axis=0))...]
    all_to_all x0 -> x1, starting transfers between devices: none -> 6.91 us  [on_device(): lax.all_to_all(jnp.stack(jnp.split(grad_q, lax.axis_size('ctx'), axis=0))...]
  transfers between devices with their start and end apart: 8 -> 9, of which waited for: 6 -> 6; matrix products, arithmetic and copies ran while one was open for 7% -> 52% of each run, Pallas kernels for 0% -> 0%
where the time goes in v1:
time: 687 us; the launch traced here: 680 us
  local copies, waits for them, and re-layouts  202 us (29%)
  matrix products  146 us (21%)
  other arithmetic  122 us (18%)
  waiting for transfers between devices  80.2 us (12%)
  starting transfers between devices  56.7 us (8%)
  blocking collectives  56.6 us (8%)
  between operations  15.1 us (2%)
    scatter-add x8, other arithmetic, backward_one_group(): dk_sum.at[flat_ids].add(dk_slots)  50.7 us
    scatter-add x8, other arithmetic, backward_one_group(): dv_sum.at[flat_ids].add(dv_slots)  49.8 us
    sub x16, matrix products, softmax_rows(): exponent = jnp.exp(scores - row_max)  47.9 us
    gather x32, local copies, waits for them, and re-layouts, gather_slots(): picked = blocks_in[id_group]  43.6 us
    unnamed x89, local copies, waits for them, and re-layouts  36.8 us
    unnamed x2, waiting for transfers between devices  36.4 us
    all_gather x1, blocking collectives, on_device(): columns = lax.all_gather(gain_terms, 'ctx', axis=1, tiled=True)  28.5 us
    all_gather x1, blocking collectives, on_device(): all_gains = lax.all_gather(gains, 'dp', axis=1, tiled=True)  28.1 us
  transfers between devices with their start and end apart: 9, of which 6 were waited for; matrix products, arithmetic and copies ran while one was open for 52% of the time, Pallas kernels for 0%

profile of v1, /device:TPU:2, one launch (start us, length us, event | category | flops | bytes accessed | tf_op | source)
XLA Modules:
  0.0 680.0 jit_solution(9676478907686149390)
XLA Ops:
  10.1 7.6 %all-to-all-start.1 = ((bf16[128,32,128]{2,0,1:T(8,128)(2,1)}), bf16[128,32,128]{2,0,1:T(8,128)(2,1)S(1)}, u32[]{:S(2)}, u32[]{:S(2)}) async-start(bf16[128,32,128]{2,0,1:T(8,128)(2,1)} %copy.219), calls=%async_computation.1 | async-start | bytes 2097152 | tf_op jit(solution)/shard_map/all_to_all | solution.py:189
  19.8 12.4 %all-to-all-done.1 = bf16[128,32,128]{2,0,1:T(8,128)(2,1)S(1)} async-done(((bf16[128,32,128]{2,0,1:T(8,128)(2,1)}), bf16[128,32,128]{2,0,1:T(8,128)(2,1)S(1)}, u32[]{:S(2)}, u32[]{:S(2)}) %all-to-all-start.1) | async-done | bytes 1048608 | tf_op jit(solution)/shard_map/all_to_all | solution.py:189
  32.2 6.6 all-to-all-start.2
  38.8 28.1 %all_gather.6 = f32[2,4096]{1,0:T(2,128)S(1)} all-gather(f32[2,512]{1,0:T(2,128)S(1)} %copy-done.23), channel_id=1, replica_groups=mesh['dp'=8,'ctx'=32] {'dp'}, dimensions={1}, use_global_device_ids=true | all-gather | bytes 36864 | tf_op jit(solution)/shard_map/all_gather | solution.py:184
  68.5 7.4 %all-to-all-start = ((bf16[128,32,128]{0,2,1:T(8,128)(2,1)}), bf16[128,32,128]{0,2,1:T(8,128)(2,1)S(1)}, u32[]{:S(2)}, u32[]{:S(2)}) async-start(bf16[128,32,128]{0,2,1:T(8,128)(2,1)} %bitcast.508), calls=%async_computation | async-start | bytes 2097152 | tf_op jit(solution)/shard_map/all_to_all | solution.py:191
  80.9 9.4 %all-to-all-done = bf16[128,32,128]{0,2,1:T(8,128)(2,1)S(1)} async-done(((bf16[128,32,128]{0,2,1:T(8,128)(2,1)}), bf16[128,32,128]{0,2,1:T(8,128)(2,1)S(1)}, u32[]{:S(2)}, u32[]{:S(2)}) %all-to-all-start) | async-done | bytes 1048608 | tf_op jit(solution)/shard_map/all_to_all | solution.py:191
  90.3 6.9 %all-to-all-start.4 = ((bf16[128,32,128]{2,0,1:T(8,128)(2,1)}), bf16[128,32,128]{2,0,1:T(8,128)(2,1)}, u32[]{:S(2)}, u32[]{:S(2)}) async-start(bf16[128,32,128]{2,0,1:T(8,128)(2,1)} %copy.231), calls=%async_computation.4 | async-start | bytes 2097152 | tf_op jit(solution)/shard_map/all_to_all | solution.py:213
  108.6 3.2 all-to-all-done.4
  117.8 76.8 %while.24 = (s32[]{:T(128)}, bf16[8,4,128,1,128]{4,2,1,0,3:T(8,128)(2,1)}, s32[8,4,8]{2,1,0:T(4,128)S(1)}, bf16[32,128,1,128]{3,1,0,2:T(8,128)(2,1)S(1)}, pred[8...) while((s32[]{:T(128)}, ...), condition=%wide.region_4.5_spmd, body=%wide.region_1.4_spmd.sunk | while | flops 271648864 | bytes 11297869 | solution.py:82
  121.4 3.0 fusion.132
  131.0 3.0 fusion.132
  140.6 3.0 fusion.132
  150.2 3.0 fusion.132
  159.8 3.0 fusion.132
  169.4 3.0 fusion.132
  179.0 3.0 fusion.132
  188.6 3.0 fusion.132
  202.9 6.9 %all-to-all-start.3 = ((bf16[32,128,128]{2,1,0:T(8,128)(2,1)}), bf16[32,128,128]{2,1,0:T(8,128)(2,1)}, u32[]{:S(2)}, u32[]{:S(2)}) async-start(bf16[32,128,128]{2,1,0:T(8,128)(2,1)} %scatter_fusion.2), calls=%async_computation.3 | async-start | bytes 2097152 | tf_op jit(solution)/shard_map/all_to_all | solution.py:210
  212.6 3.4 fusion.56
  224.7 291.2 %while.25 = (s32[]{:T(128)}, f32[32,128,1,128]{3,1,0,2:T(8,128)}, f32[32,128,1,128]{3,1,0,2:T(8,128)}, f32[8,4,128,1,128]{4,2,1,0,3:T(8,128)}, s32[8,4,8]{2,1,0:...) while((s32[]{:T(128)}, f32[32,128,1,128]{3,1,0,2:T(8,128)}, ...), condition=%wide.region_15.16_spmd, body=%wide.region_10.15_spmd.sunk | while | flops 677972160 | bytes 57460872 | solution.py:144
  229.6 3.0 fusion.145
  237.3 2.8 convolution_bitcast_fusion.5
  241.9 6.2 scatter_fusion.1
  249.0 3.1 multiply_bitcast_fusion.2
  254.1 6.4 scatter_fusion
  266.0 3.0 fusion.145
  278.4 6.2 scatter_fusion.1
  285.4 3.1 multiply_bitcast_fusion.2
  290.4 6.3 scatter_fusion
  302.4 3.0 fusion.145
  310.0 2.8 convolution_bitcast_fusion.5
  314.7 6.2 scatter_fusion.1
  321.8 3.1 multiply_bitcast_fusion.2
  326.8 6.4 scatter_fusion
  338.8 3.0 fusion.145
  351.2 6.2 scatter_fusion.1
  358.2 3.1 multiply_bitcast_fusion.2
  363.3 6.3 scatter_fusion
  375.2 3.0 fusion.145
  387.6 6.2 scatter_fusion.1
  394.6 3.1 multiply_bitcast_fusion.2
  399.7 6.4 scatter_fusion
  411.6 3.0 fusion.145
  424.0 6.2 scatter_fusion.1
  431.0 3.1 multiply_bitcast_fusion.2
  436.1 6.3 scatter_fusion
  448.0 3.0 fusion.145
  460.3 6.2 scatter_fusion.1
  467.3 3.1 multiply_bitcast_fusion.2
  472.4 6.3 scatter_fusion
  484.3 3.0 fusion.145
  496.7 6.2 scatter_fusion.1
  503.8 3.1 multiply_bitcast_fusion.2
  508.8 6.4 scatter_fusion
  519.9 3.0 copy.267
  523.0 3.2 multiply_reduce_fusion.1
  544.5 7.5 %all-to-all-start.6 = ((bf16[32,128,128]{1,2,0:T(8,128)(2,1)}), bf16[32,128,128]{1,2,0:T(8,128)(2,1)S(1)}, u32[]{:S(2)}, u32[]{:S(2)}) async-start(bf16[32,128,128]{1,2,0:T(8,128)(2,1)} %copy.245), calls=%async_computation.6 | async-start | bytes 2097152 | tf_op jit(solution)/shard_map/all_to_all | solution.py:235
  555.1 11.3 %all-to-all-done.6 = bf16[32,128,128]{1,2,0:T(8,128)(2,1)S(1)} async-done(((bf16[32,128,128]{1,2,0:T(8,128)(2,1)}), bf16[32,128,128]{1,2,0:T(8,128)(2,1)S(1)}, u32[]{:S(2)}, u32[]{:S(2)}) %all-to-all-start.6) | async-done | bytes 1048608 | tf_op jit(solution)/shard_map/all_to_all | solution.py:235
  566.4 6.9 %all-to-all-start.5 = ((bf16[32,128,128]{2,1,0:T(8,128)(2,1)}), bf16[32,128,128]{2,1,0:T(8,128)(2,1)}, u32[]{:S(2)}, u32[]{:S(2)}) async-start(bf16[32,128,128]{2,1,0:T(8,128)(2,1)} %constant_dynamic-update-slice_fusion.2), calls=%async_computation.5 | async-start | bytes 2097152 | tf_op jit(solution)/shard_map/all_to_all | solution.py:232
  573.3 3.0 copy.268
  580.5 7.4 %all-to-all-done.5 = bf16[32,128,128]{2,1,0:T(8,128)(2,1)} async-done(((bf16[32,128,128]{2,1,0:T(8,128)(2,1)}), bf16[32,128,128]{2,1,0:T(8,128)(2,1)}, u32[]{:S(2)}, u32[]{:S(2)}) %all-to-all-start.5) | async-done | bytes 1048608 | tf_op jit(solution)/shard_map/all_to_all | solution.py:232
  587.9 6.9 %all-to-all-start.7 = ((bf16[32,128,128]{1,2,0:T(8,128)(2,1)}), bf16[32,128,128]{1,2,0:T(8,128)(2,1)}, u32[]{:S(2)}, u32[]{:S(2)}) async-start(bf16[32,128,128]{1,2,0:T(8,128)(2,1)} %copy.249), calls=%async_computation.7 | async-start | bytes 2097152 | tf_op jit(solution)/shard_map/all_to_all | solution.py:236
  595.4 28.5 %all-gather = bf16[2,1,4096]{2,1,0:T(2,128)(2,1)S(1)} all-gather(bf16[2,1,128]{2,1,0:T(2,128)(2,1)S(1)} %pad_maximum_fusion), channel_id=2, replica_groups=mesh['dp'=8,'ctx'=32] {'ctx'}, dimensions={2}, use_global_device_ids=true | all-gather | bytes 16896 | tf_op jit(solution)/shard_map/all_gather | solution.py:244
  625.4 36.4 %reduce-scatter.4.cloned.1.call-done = bf16[512,2]{1,0:T(8,128)(2,1)} async-done(((bf16[4096,2]{1,0:T(8,128)(2,1)}), bf16[512,2]{1,0:T(8,128)(2,1)}) %reduce-scatter.4.cloned.1.call-update) | async-done | bytes 2064
  (469 shorter events, 278.8 us)
Async XLA Ops:
  8.8 9.6 %copy-start.16 = (bf16[1,128,4096]{2,1,0:T(8,128)(2,1)S(1)}, bf16[1,128,4096]{2,1,0:T(8,128)(2,1)}, u32[]{:S(2)}) copy-start(bf16[1,128,4096]{2,1,0:T(8,128)(2,1)} %param.13) | copy-start | bytes 3145732
  10.1 22.1 %all-to-all-start.1 = ((bf16[128,32,128]{2,0,1:T(8,128)(2,1)}), bf16[128,32,128]{2,0,1:T(8,128)(2,1)S(1)}, u32[]{:S(2)}, u32[]{:S(2)}) async-start(bf16[128,32,128]{2,0,1:T(8,128)(2,1)} %copy.219), calls=%async_computation.1 | async-start | bytes 2097152 | tf_op jit(solution)/shard_map/all_to_all | solution.py:189
  18.4 20.4 %copy-start.23 = (f32[2,512]{1,0:T(2,128)S(1)}, f32[2,512]{1,0:T(2,128)}, u32[]{:S(2)}) copy-start(f32[2,512]{1,0:T(2,128)} %param.16) | copy-start | bytes 12292
  18.4 48.4 %copy-start.21 = (s32[1,32,3]{1,0,2:T(1,128)S(1)}, s32[1,32,3]{1,0,2:T(1,128)}, u32[]{:S(2)}) copy-start(s32[1,32,3]{1,0,2:T(1,128)} %param.19) | copy-start | bytes 1156
  19.7 47.1 %copy-start.17 = (bf16[1,128,4096]{2,1,0:T(8,128)(2,1)S(1)}, bf16[1,128,4096]{2,1,0:T(8,128)(2,1)}, u32[]{:S(2)}) copy-start(bf16[1,128,4096]{2,1,0:T(8,128)(2,1)} %param.14) | copy-start | bytes 3145732
  32.2 84.1 %copy-start.6 = (bf16[128,32,128]{2,0,1:T(8,128)(2,1)}, bf16[128,32,128]{2,0,1:T(8,128)(2,1)S(1)}, u32[]{:S(2)}) copy-start(bf16[128,32,128]{2,0,1:T(8,128)(2,1)S(1)} %all-to-all-done.1) | copy-start | bytes 3145732
  32.2 36.2 %copy-start.24 = (s32[1,2]{1,0:T(1,128)S(1)}, s32[1,2]{1,0:T(1,128)}, u32[]{:S(2)}) copy-start(s32[1,2]{1,0:T(1,128)} %param.18) | copy-start | bytes 28
  32.2 36.3 %all-to-all-start.2 = ((bf16[128,32,128]{0,2,1:T(8,128)(2,1)}), bf16[128,32,128]{0,2,1:T(8,128)(2,1)S(1)}, u32[]{:S(2)}, u32[]{:S(2)}) async-start(bf16[128,32,128]{0,2,1:T(8,128)(2,1)} %bitcast.47), calls=%async_computation.2 | async-start | bytes 2097152 | tf_op jit(solution)/shard_map/all_to_all | solution.py:190
  68.4 132.6 %copy-start.22 = (s32[2]{0:T(128)}, s32[2]{0:T(128)S(1)}, u32[]{:S(2)}) copy-start(s32[2]{0:T(128)S(1)} %fusion.88) | copy-start | bytes 28
  68.4 9.9 %copy-start.8 = (bf16[128,32,128]{0,2,1:T(8,128)(2,1)}, bf16[128,32,128]{0,2,1:T(8,128)(2,1)S(1)}, u32[]{:S(2)}) copy-start(bf16[128,32,128]{0,2,1:T(8,128)(2,1)S(1)} %all-to-all-done.2) | copy-start | bytes 3145732
  68.5 21.8 %all-to-all-start = ((bf16[128,32,128]{0,2,1:T(8,128)(2,1)}), bf16[128,32,128]{0,2,1:T(8,128)(2,1)S(1)}, u32[]{:S(2)}, u32[]{:S(2)}) async-start(bf16[128,32,128]{0,2,1:T(8,128)(2,1)} %bitcast.508), calls=%async_computation | async-start | bytes 2097152 | tf_op jit(solution)/shard_map/all_to_all | solution.py:191
  80.7 35.8 %copy-start.20 = (f32[128]{0:T(128)}, f32[128]{0:T(128)S(1)}, u32[]{:S(2)}) copy-start(f32[128]{0:T(128)S(1)} %get-tuple-element.278) | copy-start | bytes 1540
  80.7 135.3 %copy-start.18 = (f32[128]{0:T(128)}, f32[128]{0:T(128)S(1)}, u32[]{:S(2)}) copy-start(f32[128]{0:T(128)S(1)} %get-tuple-element.277) | copy-start | bytes 1540
  90.3 7.9 %copy-start.14 = (bf16[128,32,128]{0,2,1:T(8,128)(2,1)}, bf16[128,32,128]{0,2,1:T(8,128)(2,1)S(1)}, u32[]{:S(2)}) copy-start(bf16[128,32,128]{0,2,1:T(8,128)(2,1)S(1)} %all-to-all-done) | copy-start | bytes 3145732
  90.3 21.5 %all-to-all-start.4 = ((bf16[128,32,128]{2,0,1:T(8,128)(2,1)}), bf16[128,32,128]{2,0,1:T(8,128)(2,1)}, u32[]{:S(2)}, u32[]{:S(2)}) async-start(bf16[128,32,128]{2,0,1:T(8,128)(2,1)} %copy.231), calls=%async_computation.4 | async-start | bytes 2097152 | tf_op jit(solution)/shard_map/all_to_all | solution.py:213
  104.1 3.0 copy-start.15
  197.0 1.9 copy-start.1
  199.6 1.4 copy-start.2
  202.9 341.5 %all-to-all-start.3 = ((bf16[32,128,128]{2,1,0:T(8,128)(2,1)}), bf16[32,128,128]{2,1,0:T(8,128)(2,1)}, u32[]{:S(2)}, u32[]{:S(2)}) async-start(bf16[32,128,128]{2,1,0:T(8,128)(2,1)} %scatter_fusion.2), calls=%async_computation.3 | async-start | bytes 2097152 | tf_op jit(solution)/shard_map/all_to_all | solution.py:210
  212.6 4.8 copy-start.5
  216.0 1.3 copy-start.11
  235.3 1.0 copy-start
  235.3 2.0 copy-start.25
  235.3 2.0 copy-start.27
  254.0 6.4 copy-start.4
  271.7 1.0 copy-start
  271.7 2.0 copy-start.25
  271.7 2.0 copy-start.27
  290.4 6.3 copy-start.4
  308.0 1.0 copy-start
  308.1 2.0 copy-start.25
  308.1 2.0 copy-start.27
  326.8 6.4 copy-start.4
  344.5 1.0 copy-start
  344.5 2.0 copy-start.25
  344.5 2.0 copy-start.27
  363.3 6.4 copy-start.4
  380.9 1.0 copy-start
  380.9 2.0 copy-start.25
  380.9 2.0 copy-start.27
  399.7 6.4 copy-start.4
  417.3 1.0 copy-start
  417.3 2.0 copy-start.25
  417.3 2.0 copy-start.27
  436.0 6.3 copy-start.4
  453.6 1.0 copy-start
  453.7 2.0 copy-start.25
  453.7 2.0 copy-start.27
  472.4 6.4 copy-start.4
  490.0 1.0 copy-start
  490.0 2.0 copy-start.25
  490.0 2.0 copy-start.27
  508.8 6.4 copy-start.4
  519.9 3.1 copy-start.10
  519.9 3.1 copy-start.19
  544.5 21.9 %all-to-all-start.6 = ((bf16[32,128,128]{1,2,0:T(8,128)(2,1)}), bf16[32,128,128]{1,2,0:T(8,128)(2,1)S(1)}, u32[]{:S(2)}, u32[]{:S(2)}) async-start(bf16[32,128,128]{1,2,0:T(8,128)(2,1)} %copy.245), calls=%async_computation.6 | async-start | bytes 2097152 | tf_op jit(solution)/shard_map/all_to_all | solution.py:235
  566.4 6.9 %copy-start.12 = (bf16[32,128,128]{1,2,0:T(8,128)(2,1)}, bf16[32,128,128]{1,2,0:T(8,128)(2,1)S(1)}, u32[]{:S(2)}) copy-start(bf16[32,128,128]{1,2,0:T(8,128)(2,1)S(1)} %all-to-all-done.6) | copy-start | bytes 3145732
  566.4 21.5 %all-to-all-start.5 = ((bf16[32,128,128]{2,1,0:T(8,128)(2,1)}), bf16[32,128,128]{2,1,0:T(8,128)(2,1)}, u32[]{:S(2)}, u32[]{:S(2)}) async-start(bf16[32,128,128]{2,1,0:T(8,128)(2,1)} %constant_dynamic-update-slice_fusion.2), calls=%async_computation.5 | async-start | bytes 2097152 | tf_op jit(solution)/shard_map/all_to_all | solution.py:232
  573.3 3.1 copy-start.3
  579.1 15.7 %copy-start.7 = (bf16[128,32,128]{2,0,1:T(8,128)(2,1)S(1)}, bf16[128,32,128]{2,0,1:T(8,128)(2,1)}, u32[]{:S(2)}) copy-start(bf16[128,32,128]{2,0,1:T(8,128)(2,1)} %copy-done.6) | copy-start | bytes 3145732
  579.1 15.7 %copy-start.9 = (f32[32,128,128]{2,1,0:T(8,128)S(1)}, f32[32,128,128]{2,1,0:T(8,128)}, u32[]{:S(2)}) copy-start(f32[32,128,128]{2,1,0:T(8,128)} %scatter_fusion.3) | copy-start | bytes 6291460
  587.9 83.0 %all-to-all-start.7 = ((bf16[32,128,128]{1,2,0:T(8,128)(2,1)}), bf16[32,128,128]{1,2,0:T(8,128)(2,1)}, u32[]{:S(2)}, u32[]{:S(2)}) async-start(bf16[32,128,128]{1,2,0:T(8,128)(2,1)} %copy.249), calls=%async_computation.7 | async-start | bytes 2097152 | tf_op jit(solution)/shard_map/all_to_all | solution.py:236
  594.8 67.0 %reduce-scatter.4.cloned.1.call-start = ((), (), s32[]{:S(2)}) async-start(), calls=%async_computation.9 | async-start | bytes 1179648
  663.4 3.0 copy-start.13
  (8 other events, 4.6 us)
Sparse Core Ops, SparseCore 0:
  625.5 36.2 reduce-scatter.3
